TPU v7x, 32 devices: a whole 2x2x4 slice. The times are simulated.
32 devices in a mesh: dp: 8 (over y, x, core), own: 4 (over z).
Axes of the slice: x: 2, y: 2, z: 4, core: 2. Of those that a mesh axis runs over, the one named last changes fastest.
Arguments:
- grads: bfloat16 [8, 6, 8192, 128], P('dp', None, 'own'), may hold values from -6 to 6
- proj: bfloat16 [4, 3, 8192, 1024], P('own', None, 'dp'), may hold values from -0.0625 to 0.0625
- moment1: float32 [4, 3, 1024, 128], P('own', None, 'dp'), may hold values from -24 to 24
- moment2: float32 [4, 3, 1024, 128], P('own', None, 'dp'), may hold values from 0.05 to 5
- plan: int32 [6], replicated, may hold values from 0 to 3, as said below
Outputs:
- update: bfloat16 [6, 8192, 128], P(None, 'own')
- new_moment1: float32 [4, 3, 1024, 128], P('own', None, 'dp')
- new_moment2: float32 [4, 3, 1024, 128], P('own', None, 'dp')
Inputs may be any that keep to these rules, and one draw needn't show every extreme that they name: `plan`: no owner is named more than 3 times, and some owner is named exactly 3 times.
All inputs are finite; a program needn't handle non-finite values.
Results may differ from a plain program's by a relative error of at most 0.015.
Values may be sent and summed in bfloat16 or wider, within the bound.
A program may use at most 64 MiB of HBM per device.

v0:
```python
import jax
import jax.numpy as jnp
from jax import lax
from jax.sharding import PartitionSpec as P

beta_one = 0.9
beta_two = 0.999
adam_eps = 1e-08
norm_eps = 1e-06
correct_one = 1.0 - 0.9**10
correct_two = 1.0 - 0.999**10


def slot_selector(plan, owner_count, capacity):
    matrices = plan.shape[0]
    places = jnp.arange(owner_count * capacity, dtype=jnp.int32)
    owners = places // capacity
    within = places % capacity
    index = jnp.arange(matrices, dtype=jnp.int32)
    before = jnp.sum(
        ((plan[None, :] == plan[:, None]) & (index[None, :] < index[:, None])).astype(jnp.int32),
        axis=1,
    )
    chosen = (plan[None, :] == owners[:, None]) & (before[None, :] == within[:, None])
    return chosen.astype(jnp.bfloat16)


def adam_moments(rank_share, first_old, second_old):
    first_new = beta_one * first_old + (1.0 - beta_one) * rank_share
    second_new = beta_two * second_old + (1.0 - beta_two) * rank_share * rank_share
    adam_step = first_new / correct_one / (jnp.sqrt(second_new / correct_two) + adam_eps)
    return (first_new, second_new, adam_step.astype(jnp.bfloat16))


def local(grads, proj, moment1, moment2, plan):
    owner_count = lax.axis_size("own")
    replica_count = lax.axis_size("dp")
    capacity = proj.shape[1]
    own_rows = grads.shape[2]
    columns = grads.shape[3]
    rank_rows = moment1.shape[2]
    selector = slot_selector(plan, owner_count, capacity)
    outgoing = jnp.einsum(
        "sj,jdc->sdc", selector, grads[0], preferred_element_type=jnp.float32
    ).astype(jnp.bfloat16)
    group_ratio = replica_count // owner_count
    piece_rows = own_rows // replica_count
    blocked = outgoing.reshape(owner_count * capacity, replica_count, piece_rows, columns)
    pieces = lax.psum_scatter(blocked, "dp", scatter_dimension=1, tiled=True).astype(jnp.float32)
    pieces = pieces.reshape(owner_count, capacity, piece_rows, columns)
    routed = lax.all_to_all(
        pieces.astype(jnp.bfloat16), "own", split_axis=0, concat_axis=0, tiled=True
    ).astype(pieces.dtype)
    span_pos = lax.axis_index("dp") // owner_count
    marker = (jnp.arange(group_ratio, dtype=jnp.int32) == span_pos).astype(jnp.float32)
    placed = routed[:, None] * marker[None, :, None, None, None]
    placed = placed.reshape(replica_count, capacity, piece_rows, columns)
    received = lax.all_to_all(
        placed.astype(jnp.bfloat16), "dp", split_axis=0, concat_axis=0, tiled=True
    ).astype(placed.dtype)
    received = received.reshape(group_ratio, owner_count, capacity, piece_rows, columns)
    mine = lax.axis_index("dp") % group_ratio
    kept = lax.dynamic_index_in_dim(received, mine, 0, keepdims=False)
    summed = jnp.transpose(kept, (1, 0, 2, 3)).reshape(capacity, owner_count * piece_rows, columns)
    grad_half = summed.astype(jnp.bfloat16)
    projection = proj[0]
    partial_value = jnp.einsum(
        "kdr,kdc->krc", projection, grad_half, preferred_element_type=jnp.float32
    )
    first_old = moment1[0]
    second_old = moment2[0]
    rank_full = lax.psum(partial_value.astype(jnp.bfloat16), "dp").astype(jnp.float32)
    rank_start = lax.axis_index("dp") * rank_rows
    rank_share = lax.dynamic_slice_in_dim(rank_full, rank_start, rank_rows, 1)
    first_new, second_new, adam_half = adam_moments(rank_share, first_old, second_old)
    adam_full = lax.all_gather(adam_half, "dp", axis=1, tiled=True)
    rank_half = rank_full.astype(jnp.bfloat16)
    grad_norms = jnp.sum(rank_full * rank_full, axis=1)
    adam_wide = adam_full.astype(jnp.float32)
    step_norms = jnp.sum(adam_wide * adam_wide, axis=1)
    column_scale = jnp.sqrt(step_norms) / (jnp.sqrt(grad_norms) + norm_eps)
    combined = (adam_wide - column_scale[:, None, :] * rank_half.astype(jnp.float32)).astype(
        jnp.bfloat16
    )
    update_full = (
        jnp.einsum("kdr,krc->kdc", projection, combined, preferred_element_type=jnp.float32)
        + column_scale[:, None, :] * summed
    )
    update_half = update_full.astype(jnp.bfloat16)
    gathered = lax.all_gather(update_half, "dp", axis=1, tiled=True)
    gathered = gathered.reshape(capacity, owner_count, own_rows, columns)
    returned = lax.all_to_all(gathered, "own", split_axis=1, concat_axis=0, tiled=True)
    slot_rows = returned.reshape(owner_count * capacity, own_rows, columns)
    update = jnp.einsum(
        "sj,sdc->jdc", selector, slot_rows, preferred_element_type=jnp.float32
    ).astype(jnp.bfloat16)
    return (update, first_new[None], second_new[None])


def solution(mesh):
    return jax.shard_map(
        local,
        mesh=mesh,
        in_specs=(
            P("dp", None, "own", None),
            P("own", None, "dp", None),
            P("own", None, "dp", None),
            P("own", None, "dp", None),
            P(),
        ),
        out_specs=(P(None, "own", None), P("own", None, "dp", None), P("own", None, "dp", None)),
        check_vma=False,
    )
```

profile of v0, /device:TPU:25, one launch (start us, length us, event | category | flops | bytes accessed | tf_op | source)
XLA Modules:
  0.0 443.2 jit_solution(17571062850924733432)
XLA Ops:
  7.2 0.0 copy-start
  7.2 0.0 reduce-scatter.2.cloned.1.call-start
  7.2 1.0 convert_reduce_fusion
  8.2 0.8 copy-done
  9.1 13.2 %convolution_convert_fusion = bf16[12,2048,128]{2,0,1:T(8,128)(2,1)S(1)} fusion(bf16[6,2048,128]{2,1,0:T(8,128)(2,1)S(1)} %bitcast.60, s32[12]{0:T(128)S(1)} %get-tuple-element.18, s32[12]{0:T(128)S(1)} %get-tuple-element.19, s32[6]{0:T(128)S(1)} %convert_reduce_fusion, s32[6]{0:T(128)} %param.9), kind=kOutput, calls=%fused_computation.2 | convolution fusion | flops 40894680 | bytes 9437328 | tf_op jit(solution)/shard_map/sj,jdc->sdc/dot_general | solution.py:43
  22.3 4.4 %copy.37 = bf16[12,8,256,128]{3,2,0,1:T(8,128)(2,1)} copy(bf16[12,8,256,128]{3,0,2,1:T(8,128)(2,1)S(1)} %bitcast.61) | data formatting | bytes 12582912 | tf_op jit(solution)/shard_map/reshape | solution.py:48
  26.8 0.0 reduce-scatter.2.cloned.1.call-update
  26.8 62.7 %reduce-scatter.2.cloned.1.call-done = bf16[12,1,256,128]{3,2,0,1:T(8,128)(2,1)} async-done(((bf16[12,8,256,128]{3,2,0,1:T(8,128)(2,1)}), bf16[12,1,256,128]{3,2,0,1:T(8,128)(2,1)}) %reduce-scatter.2.cloned.1.call-update) | async-done | bytes 786448 | tf_op jit(solution)/shard_map/reduce_scatter | solution.py:49
  89.5 4.5 %all-to-all-start = ((bf16[4,3,256,128]{3,2,1,0:T(8,128)(2,1)}), bf16[4,3,256,128]{3,2,1,0:T(8,128)(2,1)S(1)}, u32[]{:S(2)}, u32[]{:S(2)}) async-start(bf16[4,3,256,128]{3,2,1,0:T(8,128)(2,1)} %bitcast.63), calls=%async_computation.1 | async-start | bytes 1572864 | tf_op jit(solution)/shard_map/all_to_all | solution.py:51
  94.0 0.1 mul.82
  94.1 16.9 %all-to-all-done = bf16[4,3,256,128]{3,2,1,0:T(8,128)(2,1)S(1)} async-done(((bf16[4,3,256,128]{3,2,1,0:T(8,128)(2,1)}), bf16[4,3,256,128]{3,2,1,0:T(8,128)(2,1)S(1)}, u32[]{:S(2)}, u32[]{:S(2)}) %all-to-all-start) | async-done | bytes 786464 | tf_op jit(solution)/shard_map/all_to_all | solution.py:51
  111.0 0.1 convert_element_type.58
  111.2 1.6 fusion.7
  112.8 5.5 %all-to-all-start.1 = ((bf16[8,3,256,128]{3,2,1,0:T(8,128)(2,1)}), bf16[8,3,256,128]{3,2,1,0:T(8,128)(2,1)S(1)}, u32[]{:S(2)}, u32[]{:S(2)}) async-start(bf16[8,3,256,128]{3,2,1,0:T(8,128)(2,1)} %fusion.7), calls=%async_computation.2 | async-start | bytes 3145728 | tf_op jit(solution)/shard_map/all_to_all | solution.py:58
  118.2 0.0 all-reduce.2.cloned.1.call-start
  118.2 17.5 %all-to-all-done.1 = bf16[8,3,256,128]{3,2,1,0:T(8,128)(2,1)S(1)} async-done(((bf16[8,3,256,128]{3,2,1,0:T(8,128)(2,1)}), bf16[8,3,256,128]{3,2,1,0:T(8,128)(2,1)S(1)}, u32[]{:S(2)}, u32[]{:S(2)}) %all-to-all-start.1) | async-done | bytes 1572896 | tf_op jit(solution)/shard_map/all_to_all | solution.py:58
  135.8 0.1 convert_bitcast_fusion
  135.9 0.8 copy.38
  136.7 0.8 reshape.73
  137.6 0.0 copy-start.3
  137.6 0.0 copy-start.4
  137.6 4.7 %fusion.19 = bf16[3,1024,128]{1,2,0:T(8,128)(2,1)} fusion(bf16[1,3,1024,1024]{3,2,1,0:T(8,128)(2,1)} %param.6, f32[3,1024,128]{1,2,0:T(8,128)S(1)} %reshape.73), kind=kOutput, calls=%fused_computation.20 | convolution fusion | flops 806092800 | bytes 8650752 | tf_op jit(solution)/shard_map/kdr,kdc->krc/dot_general | solution.py:67
  142.3 0.0 all-reduce.2.cloned.1.call-update
  142.3 0.0 all-gather.2.cloned.1.call-start
  142.4 0.0 copy-done.3
  142.4 0.1 copy.35
  142.5 0.0 copy-done.4
  142.5 0.1 copy.39
  142.6 56.6 %all-reduce.2.cloned.1.call-done = bf16[3,1024,128]{1,2,0:T(8,128)(2,1)} async-done(((bf16[3,1024,128]{1,2,0:T(8,128)(2,1)}), bf16[3,1024,128]{1,2,0:T(8,128)(2,1)}) %all-reduce.2.cloned.1.call-update) | async-done | bytes 786448 | tf_op jit(solution)/shard_map/psum | solution.py:72
  199.2 0.0 copy-start.2
  199.3 1.4 convert_element_type.64
  200.6 0.2 fusion.28
  200.8 11.4 %all_gather.6 = bf16[3,1024,128]{1,2,0:T(8,128)(2,1)S(1)} all-gather(bf16[3,128,128]{1,2,0:T(8,128)(2,1)S(1)} %get-tuple-element.16), channel_id=1, replica_groups=mesh['dp'=8,'own'=4] {'dp'}, dimensions={1}, use_global_device_ids=true | all-gather | bytes 884736 | tf_op jit(solution)/shard_map/all_gather | solution.py:76
  212.2 0.2 fusion.11
  212.4 0.0 copy-done.2
  212.4 0.2 multiply_reduce_fusion
  212.7 5.9 %fusion.13 = bf16[3,1024,128]{1,2,0:T(8,128)(2,1)} fusion(f32[3,1024,128]{1,2,0:T(8,128)S(1)} %reshape.73, bf16[1,3,1024,1024]{3,2,1,0:T(8,128)(2,1)} %param.6, bf16[3,1024,128]{1,2,0:T(8,128)(2,1)S(1)} %all_gather.6, f32[3,128]{1,0:T(4,128)S(1)} %add_divide_fusion, bf16[3,1024,128]{1,2,0:T(8,128)(2,1)S(1)} %copy-done.2), kind=kOutput, calls=%fused_computation.17 | convolution fusion | flops 808452096 | bytes 10225152 | tf_op jit(solution)/shard_map/kdr,krc->kdc/dot_general | solution.py:86
  218.6 0.0 all-gather.2.cloned.1.call-update
  218.6 45.4 %all-gather.2.cloned.1.call-done = bf16[3,8192,128]{1,2,0:T(8,128)(2,1)} async-done(((bf16[3,1024,128]{1,2,0:T(8,128)(2,1)}), bf16[3,8192,128]{1,2,0:T(8,128)(2,1)}) %all-gather.2.cloned.1.call-update) | async-done | bytes 6291472 | tf_op jit(solution)/shard_map/all_gather | solution.py:90
  264.0 11.1 %reshape.74 = bf16[3,4,2048,128]{2,1,3,0:T(4,128)(2,1)} reshape(bf16[3,8192,128]{1,2,0:T(8,128)(2,1)} %all-gather.2.cloned.1.call-done) | data formatting | bytes 12582912 | tf_op jit(solution)/shard_map/reshape | solution.py:91
  275.2 11.2 %copy.40 = bf16[3,4,2048,128]{3,2,0,1:T(8,128)(2,1)} copy(bf16[3,4,2048,128]{2,1,3,0:T(4,128)(2,1)} %reshape.74) | data formatting | bytes 12582912 | tf_op jit(solution)/shard_map/reshape | solution.py:91
  286.4 0.0 copy-start.5
  286.4 5.5 %all-to-all-start.2 = ((bf16[3,4,2048,128]{3,2,0,1:T(8,128)(2,1)}), bf16[3,4,2048,128]{3,2,0,1:T(8,128)(2,1)}, u32[]{:S(2)}, u32[]{:S(2)}) async-start(bf16[3,4,2048,128]{3,2,0,1:T(8,128)(2,1)} %copy.40), calls=%async_computation.3 | async-start | bytes 12582912 | tf_op jit(solution)/shard_map/all_to_all | solution.py:92
  291.9 0.8 copy.43
  292.8 0.8 copy.44
  293.6 134.3 %all-to-all-done.2 = bf16[3,4,2048,128]{3,2,0,1:T(8,128)(2,1)} async-done(((bf16[3,4,2048,128]{3,2,0,1:T(8,128)(2,1)}), bf16[3,4,2048,128]{3,2,0,1:T(8,128)(2,1)}, u32[]{:S(2)}, u32[]{:S(2)}) %all-to-all-start.2) | async-done | bytes 6291488 | tf_op jit(solution)/shard_map/all_to_all | solution.py:92
  427.9 0.0 copy-done.5
  427.9 0.0 copy-start.1
  427.9 6.7 %fusion.8 = bf16[6,2048,128]{2,0,1:T(8,128)(2,1)S(1)} fusion(bf16[12,2048,128]{2,1,0:T(8,128)(2,1)} %bitcast.15, s32[12]{0:T(128)S(1)} %get-tuple-element.18, s32[12]{0:T(128)S(1)} %get-tuple-element.19, s32[6]{0:T(128)S(1)} %convert_reduce_fusion, s32[6]{0:T(128)S(1)} %copy-done.5), kind=kOutput, calls=%fused_computation.10 | convolution fusion | flops 39321816 | bytes 9437328 | tf_op jit(solution)/shard_map/sj,sdc->jdc/dot_general | solution.py:94
  434.6 2.1 copy.42
  436.6 0.0 copy-done.1
  (4 shorter events, 0.0 us)
Async XLA Ops:
  7.2 1.9 copy-start
  7.2 82.3 %reduce-scatter.2.cloned.1.call-start = ((), (), s32[]{:S(2)}) async-start(), calls=%async_computation.4 | async-start | bytes 7077888 | tf_op jit(solution)/shard_map/reduce_scatter | solution.py:49
  89.5 21.5 %all-to-all-start = ((bf16[4,3,256,128]{3,2,1,0:T(8,128)(2,1)}), bf16[4,3,256,128]{3,2,1,0:T(8,128)(2,1)S(1)}, u32[]{:S(2)}, u32[]{:S(2)}) async-start(bf16[4,3,256,128]{3,2,1,0:T(8,128)(2,1)} %bitcast.63), calls=%async_computation.1 | async-start | bytes 1572864 | tf_op jit(solution)/shard_map/all_to_all | solution.py:51
  112.8 23.0 %all-to-all-start.1 = ((bf16[8,3,256,128]{3,2,1,0:T(8,128)(2,1)}), bf16[8,3,256,128]{3,2,1,0:T(8,128)(2,1)S(1)}, u32[]{:S(2)}, u32[]{:S(2)}) async-start(bf16[8,3,256,128]{3,2,1,0:T(8,128)(2,1)} %fusion.7), calls=%async_computation.2 | async-start | bytes 3145728 | tf_op jit(solution)/shard_map/all_to_all | solution.py:58
  118.2 81.0 %all-reduce.2.cloned.1.call-start = ((), (), s32[]{:S(2)}) async-start(), calls=%async_computation.5 | async-start | bytes 1572864 | tf_op jit(solution)/shard_map/psum | solution.py:72
  137.6 4.8 %copy-start.3 = (f32[1,3,128,128]{3,2,1,0:T(8,128)S(1)}, f32[1,3,128,128]{3,2,1,0:T(8,128)}, u32[]{:S(2)}) copy-start(f32[1,3,128,128]{3,2,1,0:T(8,128)} %param.7) | copy-start | bytes 589828
  137.6 4.9 %copy-start.4 = (f32[1,3,128,128]{3,2,1,0:T(8,128)S(1)}, f32[1,3,128,128]{3,2,1,0:T(8,128)}, u32[]{:S(2)}) copy-start(f32[1,3,128,128]{3,2,1,0:T(8,128)} %param.8) | copy-start | bytes 589828
  142.3 121.7 %all-gather.2.cloned.1.call-start = ((), (), s32[]{:S(2)}) async-start(), calls=%async_computation.6 | async-start | bytes 7077888 | tf_op jit(solution)/shard_map/all_gather | solution.py:90
  199.2 13.2 %copy-start.2 = (bf16[3,1024,128]{1,2,0:T(8,128)(2,1)S(1)}, bf16[3,1024,128]{1,2,0:T(8,128)(2,1)}, u32[]{:S(2)}) copy-start(bf16[3,1024,128]{1,2,0:T(8,128)(2,1)} %all-reduce.2.cloned.1.call-done) | copy-start | bytes 2359300
  286.4 141.5 %copy-start.5 = (s32[6]{0:T(128)S(1)}, s32[6]{0:T(128)}, u32[]{:S(2)}) copy-start(s32[6]{0:T(128)} %param.9) | copy-start | bytes 76
  286.4 141.5 %all-to-all-start.2 = ((bf16[3,4,2048,128]{3,2,0,1:T(8,128)(2,1)}), bf16[3,4,2048,128]{3,2,0,1:T(8,128)(2,1)}, u32[]{:S(2)}, u32[]{:S(2)}) async-start(bf16[3,4,2048,128]{3,2,0,1:T(8,128)(2,1)} %copy.40), calls=%async_computation.3 | async-start | bytes 12582912 | tf_op jit(solution)/shard_map/all_to_all | solution.py:92
  427.9 8.7 %copy-start.1 = (bf16[1,6,2048,128]{3,2,1,0:T(8,128)(2,1)S(1)}, bf16[1,6,2048,128]{3,2,1,0:T(8,128)(2,1)}, u32[]{:S(2)}) copy-start(bf16[1,6,2048,128]{3,2,1,0:T(8,128)(2,1)} %param.5) | copy-start | bytes 9437188
Sparse Core Ops, SparseCore 0:
  26.9 62.5 reduce-scatter.1
  142.4 56.7 all-reduce.1
  218.7 45.2 all-gather.1
where the time goes:
time: 448 us; the launch traced here: 443 us
  waiting for transfers between devices  334 us (75%)
  local copies, waits for them, and re-layouts  33.4 us (7%)
  matrix products  30.5 us (7%)
  starting transfers between devices  15.6 us (3%)
  between operations  13.9 us (3%)
  blocking collectives  11.4 us (3%)
  other arithmetic  4.88 us (1%)
    all_to_all x1, waiting for transfers between devices, local(): lax.all_to_all(gathered, 'own', split_axis=1, concat_axis=0, tiled=True)  134 us
    reduce_scatter x1, waiting for transfers between devices, local(): lax.psum_scatter(blocked, 'dp', scatter_dimension=1, tiled=True)  62.7 us
    psum x1, waiting for transfers between devices, local(): lax.psum(partial_value.astype(jnp.bfloat16), 'dp').astype(jnp.float32)  56.6 us
    all_gather x1, waiting for transfers between devices, local(): gathered = lax.all_gather(update_half, 'dp', axis=1, tiled=True)  45.4 us
    reshape x2, local copies, waits for them, and re-layouts, local(): gathered = gathered.reshape(capacity, owner_count, own_rows, columns)  22.4 us
    all_to_all x1, waiting for transfers between devices, local(): lax.all_to_all(placed.astype(jnp.bfloat16), 'dp', split_axis=0, concat_ax...  17.5 us
    all_to_all x1, waiting for transfers between devices, local(): lax.all_to_all(pieces.astype(jnp.bfloat16), 'own', split_axis=0, concat_a...  16.9 us
    dot_general x1, matrix products, local(): jnp.einsum('sj,jdc->sdc', selector, grads[0], preferred_element_type=jnp....  13.2 us
  transfers between devices with their start and end apart: 6, of which 6 were waited for; matrix products, arithmetic and copies ran while one was open for 0% of the time, Pallas kernels for 0%

commit v1 on v0

v1 whole, which is shorter than its diff:
```python
import functools
import jax
import jax.numpy as jnp
from jax import lax
from jax.experimental import pallas as pl
from jax.experimental.pallas import tpu as pltpu
from jax.sharding import PartitionSpec as P

beta_one = 0.9
beta_two = 0.999
adam_eps = 1e-08
norm_eps = 1e-06
correct_one = 1.0 - 0.9**10
correct_two = 1.0 - 0.999**10

CHUNKS = 2
F32 = jnp.float32
BF16 = jnp.bfloat16


def kernel(
    n, m, plan, grads, proj, m1, m2, out, m1_out, m2_out,
    own_half, pair_half, half_sum, chip_in, total, slot_out, slot_in, grad, weights,
    part, part_in, pair_sum, share_in, norms, norms_in, mixed, update, row_in, plane_in, picked,
    local_sem,
    s_pair, r_pair, s_chip, r_chip, s_slot, r_slot, s_row, r_row,
    s_part, r_part, s_share, r_share, s_norm, r_norm, s_mix, r_mix, s_mixf, r_mixf,
    s_back, r_back, s_home, r_home, s_out, r_out, s_outf, r_outf,
):
    mats = grads.shape[0]
    chips = n // 2
    piece = grads.shape[3]
    chunk = piece // CHUNKS
    cap = m1.shape[0]
    rank_rows = m1.shape[1]
    cols = m1.shape[2]
    rank = n * rank_rows
    dp = lax.axis_index("dp")
    own = lax.axis_index("own")
    core = lax.rem(dp, 2)
    chip = lax.div(dp, 2)
    other = 1 - core
    partner = (2 * chip + other, own)

    def at_chip(which):
        return (2 * which + core, own)

    def remote(src, dst, send, recv, device):
        return pltpu.make_async_remote_copy(
            src_ref=src, dst_ref=dst, send_sem=send, recv_sem=recv,
            device_id=device, device_id_type=pl.DeviceIdType.MESH,
        )

    def rows(ch):
        return pl.ds(ch * chunk, chunk)

    load_half = pltpu.make_async_copy(grads.at[:, core], own_half, local_sem.at[0])
    load_half.start()
    load_proj = pltpu.make_async_copy(proj, weights, local_sem.at[1])
    load_proj.start()

    owner = [plan[j] for j in range(mats)]
    place = []
    for j in range(mats):
        before = jnp.int32(0)
        for i in range(j):
            before = before + jnp.where(owner[i] == owner[j], 1, 0)
        place.append(owner[j] * cap + before)

    def occupant(slot):
        index = jnp.int32(0)
        valid = jnp.int32(0)
        for j in range(mats):
            here = place[j] == slot
            index = jnp.where(here, j, index)
            valid = jnp.where(here, 1, valid)
        return index, valid.astype(F32)

    barrier = pltpu.get_barrier_semaphore()
    for d in range(1, n):
        pl.semaphore_signal(
            barrier, inc=1, device_id=(lax.rem(dp + d, n), own),
            device_id_type=pl.DeviceIdType.MESH,
        )
    for d in range(1, m):
        pl.semaphore_signal(
            barrier, inc=1, device_id=(dp, lax.rem(own + d, m)),
            device_id_type=pl.DeviceIdType.MESH,
        )
    pl.semaphore_wait(barrier, n - 1 + m - 1)

    sends = []

    pair = []
    for ch in range(CHUNKS):
        c = remote(
            grads.at[:, other, :, rows(ch)], pair_half.at[:, :, rows(ch)],
            s_pair.at[ch], r_pair.at[ch], partner,
        )
        c.start()
        pair.append(c)
    load_half.wait()
    over_chips = {}
    for ch in range(CHUNKS):
        pair[ch].wait_recv()

        @pl.loop(0, mats * chips)
        def _(i):
            j = lax.div(i, chips)
            t = lax.rem(i, chips)
            half_sum[t, j, rows(ch)] = (
                own_half[j, t, rows(ch)].astype(F32) + pair_half[j, t, rows(ch)].astype(F32)
            ).astype(BF16)

        for d in range(1, chips):
            to = lax.rem(chip + d, chips)
            c = remote(
                half_sum.at[to, :, rows(ch)], chip_in.at[d - 1, :, rows(ch)],
                s_chip.at[ch, d], r_chip.at[ch, d], at_chip(to),
            )
            c.start()
            over_chips[ch, d] = c
    sends += pair + list(over_chips.values())

    to_owner = {}
    for ch in range(CHUNKS):
        for d in range(1, chips):
            over_chips[ch, d].wait_recv()

        @pl.loop(0, mats)
        def _(j):
            acc = half_sum[chip, j, rows(ch)].astype(F32)
            for d in range(1, chips):
                acc = acc + chip_in[d - 1, j, rows(ch)].astype(F32)
            total[j, rows(ch)] = acc.astype(BF16)

        for dz in list(range(1, m)) + [0]:
            to = lax.rem(own + dz, m)
            for k in range(cap):
                index, valid = occupant(to * cap + k)
                value = (total[index, rows(ch)].astype(F32) * valid).astype(BF16)
                if dz == 0:
                    slot_in[0, k, rows(ch)] = value
                else:
                    slot_out[dz - 1, k, rows(ch)] = value
            if dz > 0:
                c = remote(
                    slot_out.at[dz - 1, :, rows(ch)], slot_in.at[dz, :, rows(ch)],
                    s_slot.at[ch, dz], r_slot.at[ch, dz], (dp, to),
                )
                c.start()
                to_owner[ch, dz] = c
    sends += list(to_owner.values())

    guarded = []
    for ch in range(CHUNKS):
        for dz in range(m):
            if dz > 0:
                to_owner[ch, dz].wait_recv()
            plane = lax.rem(own + m - dz, m)
            d = lax.rem(plane + chips - chip, chips)
            c = remote(
                slot_in.at[dz, :, rows(ch)], grad.at[:, chip, rows(ch)],
                s_row.at[ch, dz], r_row.at[ch, d], at_chip(plane),
            )

            @pl.when(d != 0)
            def _():
                c.start()

            @pl.when(d == 0)
            def _():
                for k in range(cap):
                    grad[k, chip, rows(ch)] = slot_in[dz, k, rows(ch)]

            guarded.append((d, c))
    for ch in range(CHUNKS):
        for d in range(1, chips):
            remote(
                slot_in.at[0, :, rows(ch)], grad.at[:, chip, rows(ch)],
                s_row.at[ch, 0], r_row.at[ch, d], at_chip(chip),
            ).wait_recv()

    load_proj.wait()
    parts = []
    for k in range(cap):
        g = grad[k].reshape(chips * piece, cols)
        w = weights[k].reshape(chips * piece, rank)
        value = lax.dot_general(g, w, (((0,), (0,)), ((), ())), preferred_element_type=F32)
        value = value.T.astype(BF16)
        for t in range(chips):
            for s in range(2):
                at = (2 * t + s) * rank_rows
                part[s, k, t] = value[at : at + rank_rows]
        c = remote(part.at[other, k], part_in.at[k], s_part.at[k], r_part.at[k], partner)
        c.start()
        parts.append(c)
    shares = {}
    for k in range(cap):
        parts[k].wait_recv()
        for t in range(chips):
            pair_sum[k, t] = (part[core, k, t].astype(F32) + part_in[k, t].astype(F32)).astype(BF16)
        for d in range(1, chips):
            to = lax.rem(chip + d, chips)
            c = remote(
                pair_sum.at[k, to], share_in.at[k, d - 1],
                s_share.at[k, d], r_share.at[k, d], at_chip(to),
            )
            c.start()
            shares[k, d] = c
    sends += parts + list(shares.values())

    rank_half = []
    adam = []
    for k in range(cap):
        for d in range(1, chips):
            shares[k, d].wait_recv()
        value = pair_sum[k, chip].astype(F32)
        for d in range(1, chips):
            value = value + share_in[k, d - 1].astype(F32)
        first = beta_one * m1[k] + (1.0 - beta_one) * value
        second = beta_two * m2[k] + (1.0 - beta_two) * value * value
        m1_out[k] = first
        m2_out[k] = second
        step = first / correct_one / (jnp.sqrt(second / correct_two) + adam_eps)
        step = step.astype(BF16)
        wide = step.astype(F32)
        norms[k] = jnp.sum(value * value, axis=0, keepdims=True)
        norms[cap + k] = jnp.sum(wide * wide, axis=0, keepdims=True)
        rank_half.append(value.astype(BF16))
        adam.append(wide)
    across = []
    for d in range(1, n):
        c = remote(
            norms, norms_in.at[d - 1], s_norm.at[d], r_norm.at[d], (lax.rem(dp + d, n), own)
        )
        c.start()
        across.append(c)
    sends += across
    for c in across:
        c.wait_recv()
    sums = norms[...]
    for d in range(1, n):
        sums = sums + norms_in[d - 1]
    scale = []
    for k in range(cap):
        scale.append(jnp.sqrt(sums[cap + k]) / (jnp.sqrt(sums[k]) + norm_eps))
        mixed[k, dp] = (adam[k] - scale[k] * rank_half[k].astype(F32)).astype(BF16)
    mix = []
    for d in range(1, chips):
        to = lax.rem(chip + d, chips)
        c = remote(mixed.at[:, dp], mixed.at[:, dp], s_mix.at[d], r_mix.at[d], at_chip(to))
        c.start()
        mix.append(c)
    forward = []
    c = remote(mixed.at[:, dp], mixed.at[:, dp], s_mixf.at[0], r_mixf.at[0], partner)
    c.start()
    forward.append(c)
    for d in range(1, chips):
        mix[d - 1].wait_recv()
        at = 2 * lax.rem(chip + chips - d, chips) + core
        c = remote(mixed.at[:, at], mixed.at[:, at], s_mixf.at[d], r_mixf.at[d], partner)
        c.start()
        forward.append(c)
    for c in forward:
        c.wait_recv()
    sends += mix + forward

    back = {}
    for ch in range(CHUNKS):
        for k in range(cap):
            w = weights[k, :, rows(ch)].reshape(chips * chunk, rank)
            c_full = mixed[k].reshape(rank, cols)
            value = jnp.dot(w, c_full, preferred_element_type=F32)
            g = grad[k, :, rows(ch)].reshape(chips * chunk, cols).astype(F32)
            value = (value + scale[k] * g).astype(BF16)
            for t in range(chips):
                update[t, k, rows(ch)] = value[t * chunk : (t + 1) * chunk]
        for k in range(cap):
            row_in[chip, k, rows(ch)] = update[chip, k, rows(ch)]
        for d in range(1, chips):
            to = lax.rem(chip + d, chips)
            c = remote(
                update.at[to, :, rows(ch)], row_in.at[chip, :, rows(ch)],
                s_back.at[ch, d], r_back.at[ch, d], at_chip(to),
            )
            c.start()
            back[ch, d] = c
    sends += list(back.values())

    home = {}
    for ch in range(CHUNKS):
        for d in range(1, chips):
            back[ch, d].wait_recv()
        for dz in range(1, m):
            to = lax.rem(own + dz, m)
            c = remote(
                row_in.at[to, :, rows(ch)], plane_in[ch].at[own],
                s_home.at[ch, dz], r_home.at[ch, dz], (dp, to),
            )
            c.start()
            home[ch, dz] = c
        for k in range(cap):
            plane_in[ch][own, k] = row_in[own, k, rows(ch)]
    sends += list(home.values())

    gather = {}
    copies = []
    handed = {}
    for ch in range(CHUNKS):
        for dz in range(1, m):
            home[ch, dz].wait_recv()
        for j in range(mats):
            slot = place[j]
            picked[j, rows(ch)] = plane_in[ch][lax.div(slot, cap), lax.rem(slot, cap)]
        for d in range(1, chips):
            to = lax.rem(chip + d, chips)
            c = remote(
                picked.at[:, rows(ch)], out.at[:, core, chip, rows(ch)],
                s_out.at[ch, d], r_out.at[ch, d], at_chip(to),
            )
            c.start()
            gather[ch, d] = c
        c = remote(
            picked.at[:, rows(ch)], out.at[:, core, chip, rows(ch)],
            s_outf.at[ch, 0], r_outf.at[ch, 0], partner,
        )
        c.start()
        handed[ch, 0] = c
        c = pltpu.make_async_copy(
            picked.at[:, rows(ch)], out.at[:, core, chip, rows(ch)], local_sem.at[2 + ch]
        )
        c.start()
        copies.append(c)
    for ch in range(CHUNKS):
        for d in range(1, chips):
            gather[ch, d].wait_recv()
            source = lax.rem(chip + chips - d, chips)
            block = out.at[:, core, source, rows(ch)]
            c = remote(block, block, s_outf.at[ch, d], r_outf.at[ch, d], partner)
            c.start()
            handed[ch, d] = c
    for c in handed.values():
        c.wait_recv()
    sends += list(gather.values()) + list(handed.values())
    for c in copies:
        c.wait()
    for c in sends:
        c.wait_send()
    for d, c in guarded:

        @pl.when(d != 0)
        def _():
            c.wait_send()


def local(grads, proj, moment1, moment2, plan):
    n = lax.axis_size("dp")
    m = lax.axis_size("own")
    chips = n // 2
    mats, own_rows, cols = grads.shape[1:]
    cap, held_rows, rank = proj.shape[1:]
    rank_rows = moment1.shape[2]
    piece = held_rows // chips
    g = grads.reshape(mats, 2, chips, piece, cols)
    w = proj.reshape(cap, chips, piece, rank)
    vmem = pl.BlockSpec(memory_space=pltpu.VMEM)
    anywhere = pl.BlockSpec(memory_space=pl.ANY)
    dma = pltpu.SemaphoreType.DMA
    ch = CHUNKS
    share = (cap, rank_rows, cols)
    update, first, second = pl.pallas_call(
        functools.partial(kernel, n, m),
        out_shape=(
            jax.ShapeDtypeStruct(g.shape, BF16),
            jax.ShapeDtypeStruct(share, F32),
            jax.ShapeDtypeStruct(share, F32),
        ),
        in_specs=[pl.BlockSpec(memory_space=pltpu.SMEM), anywhere, anywhere, vmem, vmem],
        out_specs=(anywhere, vmem, vmem),
        scratch_shapes=[
            pltpu.VMEM((mats, chips, piece, cols), BF16),
            pltpu.VMEM((mats, chips, piece, cols), BF16),
            pltpu.VMEM((chips, mats, piece, cols), BF16),
            pltpu.VMEM((chips - 1, mats, piece, cols), BF16),
            pltpu.VMEM((mats, piece, cols), BF16),
            pltpu.VMEM((m - 1, cap, piece, cols), BF16),
            pltpu.VMEM((m, cap, piece, cols), BF16),
            pltpu.VMEM((cap, chips, piece, cols), BF16),
            pltpu.VMEM((cap, chips, piece, rank), BF16),
            pltpu.VMEM((2, cap, chips, rank_rows, cols), BF16),
            pltpu.VMEM((cap, chips, rank_rows, cols), BF16),
            pltpu.VMEM((cap, chips, rank_rows, cols), BF16),
            pltpu.VMEM((cap, chips - 1, rank_rows, cols), BF16),
            pltpu.VMEM((2 * cap, 1, cols), F32),
            pltpu.VMEM((n - 1, 2 * cap, 1, cols), F32),
            pltpu.VMEM((cap, n, rank_rows, cols), BF16),
            pltpu.VMEM((chips, cap, piece, cols), BF16),
            pltpu.VMEM((chips, cap, piece, cols), BF16),
            [pltpu.VMEM((m, cap, piece // ch, cols), BF16)] * ch,
            pltpu.VMEM((mats, piece, cols), BF16),
            dma((2 + ch,)),
            dma((ch,)), dma((ch,)),
            dma((ch, chips)), dma((ch, chips)),
            dma((ch, m)), dma((ch, m)),
            dma((ch, m)), dma((ch, chips)),
            dma((cap,)), dma((cap,)),
            dma((cap, chips)), dma((cap, chips)),
            dma((n,)), dma((n,)),
            dma((chips,)), dma((chips,)),
            dma((chips,)), dma((chips,)),
            dma((ch, chips)), dma((ch, chips)),
            dma((ch, m)), dma((ch, m)),
            dma((ch, chips)), dma((ch, chips)),
            dma((ch, chips)), dma((ch, chips)),
        ],
        compiler_params=pltpu.CompilerParams(collective_id=0, has_side_effects=True),
    )(plan, g, w, moment1[0], moment2[0])
    return (update.reshape(mats, own_rows, cols), first[None], second[None])


def solution(mesh):
    return jax.shard_map(
        local,
        mesh=mesh,
        in_specs=(
            P("dp", None, "own", None),
            P("own", None, "dp", None),
            P("own", None, "dp", None),
            P("own", None, "dp", None),
            P(),
        ),
        out_specs=(P(None, "own", None), P("own", None, "dp", None), P("own", None, "dp", None)),
        check_vma=False,
    )
```

time: 448 us -> 113 us (0.25)
  waiting for transfers between devices: 334 us -> 0 us
  Pallas kernels: 0 us -> 107 us
  matrix products: 30.5 us -> 0 us
  local copies, waits for them, and re-layouts: 33.4 us -> 5.17 us
  starting transfers between devices: 15.6 us -> 0 us
  between operations: 13.9 us -> 0.66 us
  blocking collectives: 11.4 us -> 0 us
  other arithmetic: 4.88 us -> 0 us
    all_to_all x3 -> x0, waiting for transfers between devices: 169 us -> none  [the longest x1 134 us: local(): lax.all_to_all(gathered, 'own', split_axis=1, concat_axis=0, tiled=True)]
    pallas_call x0 -> x1, Pallas kernels: none -> 107 us  [local(): pl.pallas_call(functools.partial(kernel, n, m), out_shape=(jax.ShapeDtype...]
    reduce_scatter x1 -> x0, waiting for transfers between devices: 62.7 us -> none  [local(): lax.psum_scatter(blocked, 'dp', scatter_dimension=1, tiled=True)]
    psum x1 -> x0, waiting for transfers between devices: 56.6 us -> none  [local(): lax.psum(partial_value.astype(jnp.bfloat16), 'dp').astype(jnp.float32)]
    all_gather x1 -> x0, waiting for transfers between devices: 45.4 us -> none  [local(): gathered = lax.all_gather(update_half, 'dp', axis=1, tiled=True)]
    dot_general x4 -> x0, matrix products: 30.5 us -> none  [the longest x1 13.2 us: local(): jnp.einsum('sj,jdc->sdc', selector, grads[0], preferred_element_type=jnp....]
    reshape x4 -> x0, local copies, waits for them, and re-layouts: 27.6 us -> none  [the longest x2 22.4 us: local(): gathered = gathered.reshape(capacity, owner_count, own_rows, columns)]
    all_to_all x3 -> x0, starting transfers between devices: 15.5 us -> none  [the longest x1 5.54 us: local(): lax.all_to_all(gathered, 'own', split_axis=1, concat_axis=0, tiled=True)]
  transfers between devices with their start and end apart: 6 -> 0, of which waited for: 6 -> 0; matrix products, arithmetic and copies ran while one was open for 0% -> 0% of each run, Pallas kernels for 0% -> 0%
where the time goes in v1:
time: 113 us
  Pallas kernels  107 us (95%)
  local copies, waits for them, and re-layouts  5.17 us (5%)
    pallas_call x1, Pallas kernels, local(): pl.pallas_call(functools.partial(kernel, n, m), out_shape=(jax.ShapeDtype...  107 us
    unnamed x7, local copies, waits for them, and re-layouts  5.17 us

profile of v1, /device:TPU:25, one launch (start us, length us, event | category | flops | bytes accessed | tf_op | source)
XLA Modules:
  0.0 112.5 jit_solution(11088908678963107659)
XLA Ops:
  0.6 106.7 %shard_map.76 = (bf16[6,2,4,256,128]{4,3,2,1,0:T(8,128)(2,1)}, f32[3,128,128]{2,1,0:T(8,128)}, f32[3,128,128]{2,1,0:T(8,128)}) custom-call(s32[6]{0:T(128)} %plan.1, bf16[6,2,4,256,128]{4,3,2,1,0:T(8,128)(2,1)} %bitcast.8, bf16[3,4,256,1024]{3,2,1,0:T(8,128)(2,1)} %bitcast.7, f32[3,128,128]{2,1,0:T(8,128)} %bitcast.12, f32[3,128,128]{2,1,0:T(8,128)} %bitcast.13), custom_call_target="tpu_custom_call" | custom-call | tf_op jit(solution)/shard_map/pallas_call | solution.py:372
  107.3 0.0 copy-start.1
  107.3 0.0 copy-start
  107.3 3.8 %copy.11 = bf16[6,2048,128]{2,1,0:T(8,128)(2,1)} copy(bf16[6,2048,128]{2,1,0:T(8,128)(2,1)} %bitcast.9) | data formatting | bytes 6291456
  111.1 0.0 copy-done.1
  111.2 0.7 copy.12
  111.8 0.0 copy-done
  111.8 0.7 copy.13
Async XLA Ops:
  107.3 3.8 %copy-start.1 = (f32[3,128,128]{2,1,0:T(8,128)S(1)}, f32[3,128,128]{2,1,0:T(8,128)}, u32[]{:S(2)}) copy-start(f32[3,128,128]{2,1,0:T(8,128)} %get-tuple-element.7) | copy-start | bytes 589828
  107.3 4.5 %copy-start = (f32[3,128,128]{2,1,0:T(8,128)S(1)}, f32[3,128,128]{2,1,0:T(8,128)}, u32[]{:S(2)}) copy-start(f32[3,128,128]{2,1,0:T(8,128)} %get-tuple-element.8) | copy-start | bytes 589828

commit v2 on v1

--- a/solution.py
+++ b/solution.py
@@ -13,14 +13,14 @@
 correct_one = 1.0 - 0.9**10
 correct_two = 1.0 - 0.999**10
 
-CHUNKS = 2
+CHUNKS = 4
 F32 = jnp.float32
 BF16 = jnp.bfloat16
 
 
 def kernel(
     n, m, plan, grads, proj, m1, m2, out, m1_out, m2_out,
-    own_half, pair_half, half_sum, chip_in, total, slot_out, slot_in, grad, weights,
+    own_half, pair_half, half_sum, chip_in, slot_out, slot_in, grad, weights,
     part, part_in, pair_sum, share_in, norms, norms_in, mixed, update, row_in, plane_in, picked,
     local_sem,
     s_pair, r_pair, s_chip, r_chip, s_slot, r_slot, s_row, r_row,
@@ -51,6 +51,24 @@
             device_id=device, device_id_type=pl.DeviceIdType.MESH,
         )
 
+    bits = chips.bit_length() - 1
+
+    def flip(which, mask):
+        for b in range(bits):
+            if mask >> b & 1:
+                which = which + (1 << b) * (1 - 2 * lax.rem(lax.div(which, 1 << b), 2))
+        return which
+
+    groups = []
+    for order, low, high in (
+        (list(range(bits)), 0, mats // 2),
+        (list(range(bits))[::-1], mats // 2, mats),
+    ):
+        groups.append((order, pl.ds(low, high - low)))
+
+    def subsets(free):
+        return [mask for mask in range(chips) if all(b in free for b in range(bits) if mask >> b & 1)]
+
     def rows(ch):
         return pl.ds(ch * chunk, chunk)
 
@@ -101,44 +119,57 @@
         pair.append(c)
     load_half.wait()
     over_chips = {}
+
+    def send_chips(ch, at, step):
+        order, span = groups[at]
+        for mask in subsets(order[step + 1 :]):
+            full = mask | 1 << order[step]
+            c = remote(
+                half_sum.at[full, span, rows(ch)], chip_in.at[step, mask, span, rows(ch)],
+                s_chip.at[ch, at, full], r_chip.at[ch, at, full],
+                at_chip(flip(chip, 1 << order[step])),
+            )
+            c.start()
+            over_chips[ch, at, full] = c
+
+    def take_chips(ch, at, step):
+        order, span = groups[at]
+        for mask in subsets(order[step + 1 :]):
+            over_chips[ch, at, mask | 1 << order[step]].wait_recv()
+            for j in range(span.start, span.start + span.size):
+                value = half_sum[mask, j, rows(ch)].astype(F32) + chip_in[
+                    step, mask, j, rows(ch)
+                ].astype(F32)
+                half_sum[mask, j, rows(ch)] = value.astype(BF16)
+
     for ch in range(CHUNKS):
         pair[ch].wait_recv()
-
-        @pl.loop(0, mats * chips)
-        def _(i):
-            j = lax.div(i, chips)
-            t = lax.rem(i, chips)
-            half_sum[t, j, rows(ch)] = (
-                own_half[j, t, rows(ch)].astype(F32) + pair_half[j, t, rows(ch)].astype(F32)
-            ).astype(BF16)
-
-        for d in range(1, chips):
-            to = lax.rem(chip + d, chips)
-            c = remote(
-                half_sum.at[to, :, rows(ch)], chip_in.at[d - 1, :, rows(ch)],
-                s_chip.at[ch, d], r_chip.at[ch, d], at_chip(to),
-            )
-            c.start()
-            over_chips[ch, d] = c
-    sends += pair + list(over_chips.values())
+        for mask in list(range(1, chips)) + [0]:
+            t = flip(chip, mask)
+
+            @pl.loop(0, mats)
+            def _(j):
+                half_sum[mask, j, rows(ch)] = (
+                    own_half[j, t, rows(ch)].astype(F32) + pair_half[j, t, rows(ch)].astype(F32)
+                ).astype(BF16)
+
+        for at in range(2):
+            send_chips(ch, at, 0)
+    sends += pair
 
     to_owner = {}
     for ch in range(CHUNKS):
-        for d in range(1, chips):
-            over_chips[ch, d].wait_recv()
-
-        @pl.loop(0, mats)
-        def _(j):
-            acc = half_sum[chip, j, rows(ch)].astype(F32)
-            for d in range(1, chips):
-                acc = acc + chip_in[d - 1, j, rows(ch)].astype(F32)
-            total[j, rows(ch)] = acc.astype(BF16)
+        for step in range(bits):
+            for at in range(2):
+                take_chips(ch, at, step)
+                if step + 1 < bits:
+                    send_chips(ch, at, step + 1)
 
         for dz in list(range(1, m)) + [0]:
             to = lax.rem(own + dz, m)
             for k in range(cap):
                 index, valid = occupant(to * cap + k)
-                value = (total[index, rows(ch)].astype(F32) * valid).astype(BF16)
+                value = (half_sum[0, index, rows(ch)].astype(F32) * valid).astype(BF16)
                 if dz == 0:
                     slot_in[0, k, rows(ch)] = value
                 else:
@@ -150,7 +181,7 @@
                 )
                 c.start()
                 to_owner[ch, dz] = c
-    sends += list(to_owner.values())
+    sends += list(over_chips.values()) + list(to_owner.values())
 
     guarded = []
     for ch in range(CHUNKS):
@@ -307,39 +338,65 @@
     gather = {}
     copies = []
     handed = {}
+
+    def send_gather(ch, at, step):
+        order, span = groups[at]
+        bit = 1 << order[step]
+        for mask in subsets(order[:step]):
+            block = out.at[span, core, flip(chip, mask), rows(ch)]
+            source = picked.at[span, rows(ch)] if mask == 0 else block
+            c = remote(
+                source, block, s_out.at[ch, at, mask | bit], r_out.at[ch, at, mask | bit],
+                at_chip(flip(chip, bit)),
+            )
+            c.start()
+            gather[ch, at, mask | bit] = c
+
+    def take_gather(ch, at, step):
+        order, span = groups[at]
+        bit = 1 << order[step]
+        for mask in subsets(order[:step]):
+            gather[ch, at, mask | bit].wait_recv()
+        if step + 1 < bits:
+            send_gather(ch, at, step + 1)
+        for mask in subsets(order[:step]):
+            block = out.at[span, core, flip(chip, mask | bit), rows(ch)]
+            c = remote(
+                block, block, s_outf.at[ch, at, mask | bit], r_outf.at[ch, at, mask | bit], partner
+            )
+            c.start()
+            handed[ch, at, mask | bit] = c
+
     for ch in range(CHUNKS):
         for dz in range(1, m):
             home[ch, dz].wait_recv()
         for j in range(mats):
             slot = place[j]
             picked[j, rows(ch)] = plane_in[ch][lax.div(slot, cap), lax.rem(slot, cap)]
-        for d in range(1, chips):
-            to = lax.rem(chip + d, chips)
-            c = remote(
-                picked.at[:, rows(ch)], out.at[:, core, chip, rows(ch)],
-                s_out.at[ch, d], r_out.at[ch, d], at_chip(to),
-            )
-            c.start()
-            gather[ch, d] = c
-        c = remote(
-            picked.at[:, rows(ch)], out.at[:, core, chip, rows(ch)],
-            s_outf.at[ch, 0], r_outf.at[ch, 0], partner,
-        )
-        c.start()
-        handed[ch, 0] = c
+        for at in range(2):
+            send_gather(ch, at, 0)
+        for at in range(2):
+            span = groups[at][1]
+            c = remote(
+                picked.at[span, rows(ch)], out.at[span, core, chip, rows(ch)],
+                s_outf.at[ch, at, 0], r_outf.at[ch, at, 0], partner,
+            )
+            c.start()
+            handed[ch, at, 0] = c
         c = pltpu.make_async_copy(
             picked.at[:, rows(ch)], out.at[:, core, chip, rows(ch)], local_sem.at[2 + ch]
         )
         c.start()
         copies.append(c)
-    for ch in range(CHUNKS):
-        for d in range(1, chips):
-            gather[ch, d].wait_recv()
-            source = lax.rem(chip + chips - d, chips)
-            block = out.at[:, core, source, rows(ch)]
-            c = remote(block, block, s_outf.at[ch, d], r_outf.at[ch, d], partner)
-            c.start()
-            handed[ch, d] = c
+        if ch > 0:
+            for at in range(2):
+                take_gather(ch - 1, at, 0)
+    for at in range(2):
+        take_gather(CHUNKS - 1, at, 0)
+    for step in range(1, bits):
+        for ch in range(CHUNKS):
+            for at in range(2):
+                take_gather(ch, at, step)
     for c in handed.values():
         c.wait_recv()
     sends += list(gather.values()) + list(handed.values())
@@ -368,6 +425,7 @@
     anywhere = pl.BlockSpec(memory_space=pl.ANY)
     dma = pltpu.SemaphoreType.DMA
     ch = CHUNKS
+    bits = chips.bit_length() - 1
     share = (cap, rank_rows, cols)
     update, first, second = pl.pallas_call(
         functools.partial(kernel, n, m),
@@ -382,8 +440,7 @@
             pltpu.VMEM((mats, chips, piece, cols), BF16),
             pltpu.VMEM((mats, chips, piece, cols), BF16),
             pltpu.VMEM((chips, mats, piece, cols), BF16),
-            pltpu.VMEM((chips - 1, mats, piece, cols), BF16),
-            pltpu.VMEM((mats, piece, cols), BF16),
+            pltpu.VMEM((max(bits, 1), chips, mats, piece, cols), BF16),
             pltpu.VMEM((m - 1, cap, piece, cols), BF16),
             pltpu.VMEM((m, cap, piece, cols), BF16),
             pltpu.VMEM((cap, chips, piece, cols), BF16),
@@ -401,7 +458,7 @@
             pltpu.VMEM((mats, piece, cols), BF16),
             dma((2 + ch,)),
             dma((ch,)), dma((ch,)),
-            dma((ch, chips)), dma((ch, chips)),
+            dma((ch, 2, chips)), dma((ch, 2, chips)),
             dma((ch, m)), dma((ch, m)),
             dma((ch, m)), dma((ch, chips)),
             dma((cap,)), dma((cap,)),
@@ -411,8 +468,8 @@
             dma((chips,)), dma((chips,)),
             dma((ch, chips)), dma((ch, chips)),
             dma((ch, m)), dma((ch, m)),
-            dma((ch, chips)), dma((ch, chips)),
-            dma((ch, chips)), dma((ch, chips)),
+            dma((ch, 2, chips)), dma((ch, 2, chips)),
+            dma((ch, 2, chips)), dma((ch, 2, chips)),
         ],
         compiler_params=pltpu.CompilerParams(collective_id=0, has_side_effects=True),
     )(plan, g, w, moment1[0], moment2[0])

time: 113 us -> 105 us (0.929)
  Pallas kernels: 107 us -> 99.2 us
    pallas_call x1, Pallas kernels: 107 us -> 99.2 us  [local(): pl.pallas_call(functools.partial(kernel, n, m), out_shape=(jax.ShapeDtype...]
where the time goes in v2:
time: 105 us
  Pallas kernels  99.2 us (94%)
  local copies, waits for them, and re-layouts  5.17 us (5%)
    pallas_call x1, Pallas kernels, local(): pl.pallas_call(functools.partial(kernel, n, m), out_shape=(jax.ShapeDtype...  99.2 us
    unnamed x7, local copies, waits for them, and re-layouts  5.17 us

profile of v2, /device:TPU:25, one launch (start us, length us, event | category | flops | bytes accessed | tf_op | source)
XLA Modules:
  0.0 105.0 jit_solution(6788387816082491162)
XLA Ops:
  0.6 99.2 %shard_map.76 = (bf16[6,2,4,256,128]{4,3,2,1,0:T(8,128)(2,1)}, f32[3,128,128]{2,1,0:T(8,128)}, f32[3,128,128]{2,1,0:T(8,128)}) custom-call(s32[6]{0:T(128)} %plan.1, bf16[6,2,4,256,128]{4,3,2,1,0:T(8,128)(2,1)} %bitcast.8, bf16[3,4,256,1024]{3,2,1,0:T(8,128)(2,1)} %bitcast.7, f32[3,128,128]{2,1,0:T(8,128)} %bitcast.12, f32[3,128,128]{2,1,0:T(8,128)} %bitcast.13), custom_call_target="tpu_custom_call" | custom-call | tf_op jit(solution)/shard_map/pallas_call | solution.py:430
  99.9 0.0 copy-start.1
  99.9 0.0 copy-start
  99.9 3.8 %copy.11 = bf16[6,2048,128]{2,1,0:T(8,128)(2,1)} copy(bf16[6,2048,128]{2,1,0:T(8,128)(2,1)} %bitcast.9) | data formatting | bytes 6291456
  103.7 0.0 copy-done.1
  103.7 0.7 copy.12
  104.4 0.0 copy-done
  104.4 0.7 copy.13
Async XLA Ops:
  99.9 3.8 %copy-start.1 = (f32[3,128,128]{2,1,0:T(8,128)S(1)}, f32[3,128,128]{2,1,0:T(8,128)}, u32[]{:S(2)}) copy-start(f32[3,128,128]{2,1,0:T(8,128)} %get-tuple-element.7) | copy-start | bytes 589828
  99.9 4.5 %copy-start = (f32[3,128,128]{2,1,0:T(8,128)S(1)}, f32[3,128,128]{2,1,0:T(8,128)}, u32[]{:S(2)}) copy-start(f32[3,128,128]{2,1,0:T(8,128)} %get-tuple-element.8) | copy-start | bytes 589828

commit v3 on v1

--- a/solution.py
+++ b/solution.py
@@ -13,7 +13,7 @@
 correct_one = 1.0 - 0.9**10
 correct_two = 1.0 - 0.999**10
 
-CHUNKS = 2
+CHUNKS = 4
 F32 = jnp.float32
 BF16 = jnp.bfloat16
 

time: 113 us -> 100 us (0.88)
  the two profiles are of different devices: /device:TPU:25 before, /device:TPU:11 now
where the time goes in v3:
time: 100 us
  Pallas kernels  94.3 us (94%)
  local copies, waits for them, and re-layouts  5.17 us (5%)
    pallas_call x1, Pallas kernels, local(): pl.pallas_call(functools.partial(kernel, n, m), out_shape=(jax.ShapeDtype...  94.3 us
    unnamed x7, local copies, waits for them, and re-layouts  5.17 us

profile of v3, /device:TPU:11, one launch (start us, length us, event | category | flops | bytes accessed | tf_op | source)
XLA Modules:
  0.0 100.1 jit_solution(4341712727418386320)
XLA Ops:
  0.6 94.3 %shard_map.76 = (bf16[6,2,4,256,128]{4,3,2,1,0:T(8,128)(2,1)}, f32[3,128,128]{2,1,0:T(8,128)}, f32[3,128,128]{2,1,0:T(8,128)}) custom-call(s32[6]{0:T(128)} %plan.1, bf16[6,2,4,256,128]{4,3,2,1,0:T(8,128)(2,1)} %bitcast.8, bf16[3,4,256,1024]{3,2,1,0:T(8,128)(2,1)} %bitcast.7, f32[3,128,128]{2,1,0:T(8,128)} %bitcast.12, f32[3,128,128]{2,1,0:T(8,128)} %bitcast.13), custom_call_target="tpu_custom_call" | custom-call | tf_op jit(solution)/shard_map/pallas_call | solution.py:372
  94.9 0.0 copy-start.1
  94.9 0.0 copy-start
  94.9 3.8 %copy.11 = bf16[6,2048,128]{2,1,0:T(8,128)(2,1)} copy(bf16[6,2048,128]{2,1,0:T(8,128)(2,1)} %bitcast.9) | data formatting | bytes 6291456
  98.7 0.0 copy-done.1
  98.7 0.7 copy.12
  99.4 0.0 copy-done
  99.4 0.7 copy.13
Async XLA Ops:
  94.9 3.8 %copy-start.1 = (f32[3,128,128]{2,1,0:T(8,128)S(1)}, f32[3,128,128]{2,1,0:T(8,128)}, u32[]{:S(2)}) copy-start(f32[3,128,128]{2,1,0:T(8,128)} %get-tuple-element.7) | copy-start | bytes 589828
  94.9 4.5 %copy-start = (f32[3,128,128]{2,1,0:T(8,128)S(1)}, f32[3,128,128]{2,1,0:T(8,128)}, u32[]{:S(2)}) copy-start(f32[3,128,128]{2,1,0:T(8,128)} %get-tuple-element.8) | copy-start | bytes 589828
